TPU v7x, 32 devices: a whole 2x2x4 slice. The times are simulated.
32 devices in a mesh: prompt: 8 (over y, x, core), seq: 4 (over z).
Axes of the slice: x: 2, y: 2, z: 4, core: 2. Of those that a mesh axis runs over, the one named last changes fastest.
Arguments:
- queries: bfloat16 [8, 512, 4096], P('prompt', 'seq'), may hold values from -8 to 8
- self_keys: bfloat16 [8, 512, 4096], P('prompt', 'seq'), may hold values from -8 to 8
- self_values: bfloat16 [8, 512, 4096], P('prompt', 'seq'), may hold values from -6 to 6
- cross_queries: bfloat16 [8, 512, 4096], P('prompt', 'seq')
- context: bfloat16 [8, 512, 5120], P('prompt', 'seq')
- key_weight: bfloat16 [5120, 4096], P('prompt', 'seq')
- value_weight: bfloat16 [5120, 4096], P('prompt', 'seq'), may hold values from -0.078125 to 0.078125
- lengths: int32 [8], P('prompt'), may hold values from 64 to 512, as said below
Outputs:
- attended: bfloat16 [8, 512, 4096], P('prompt', 'seq')
Inputs may be any that keep to these rules, and one draw needn't show every extreme that they name: `lengths`: each prompt's number of text tokens; some prompt has all 512.
All inputs are finite; a program needn't handle non-finite values.
Results may differ from a plain program's by a relative error of at most 0.007.
Values may be sent and summed in bfloat16 or wider, within the bound.
A program may use at most 128 MiB of HBM per device.

v0:
```python
import functools
import math

import jax
import jax.numpy as jnp
from jax import lax
from jax.experimental import pallas as pl
from jax.experimental.pallas import tpu as pltpu
from jax.sharding import PartitionSpec as P

HD = 128
CORES = 2
Q, K, V, CTX, CQ = range(5)


def kernel(
    seq_size,
    prompt_size,
    length_ref,
    q_hbm,
    k_hbm,
    v_hbm,
    cq_hbm,
    ctx_hbm,
    wk_hbm,
    wv_hbm,
    out_hbm,
    q_buf,
    k_buf,
    v_buf,
    cq_buf,
    ctx_buf,
    wk_buf,
    wv_buf,
    text_keys,
    text_values,
    self_buf,
    out_buf,
    local_sem,
    seq_send,
    seq_recv,
    text_send,
    text_recv,
    chip_send,
    chip_recv,
    pair_send,
    pair_recv,
    out_send,
    out_recv,
):
    seq = lax.axis_index("seq")
    prompt = lax.axis_index("prompt")
    chips = prompt_size // CORES
    chip = prompt // CORES
    core = prompt % CORES
    partner = chip * CORES + (1 - core)
    tokens = q_hbm.shape[0]
    width = wk_hbm.shape[1]
    depth = wk_hbm.shape[0]
    heads = width // HD
    scaling = 1.0 / math.sqrt(HD)

    def seq_peer(offset):
        return lax.rem(seq + offset, seq_size)

    def seq_source(offset):
        return lax.rem(seq + seq_size - offset, seq_size)

    def chip_peer(offset):
        return lax.rem(chip + offset, chips) * CORES + core

    def chip_source(offset):
        return lax.rem(chip + chips - offset, chips) * CORES + core

    barrier = pltpu.get_barrier_semaphore()
    for offset in range(1, seq_size):
        pl.semaphore_signal(
            barrier, inc=1, device_id={"seq": seq_peer(offset)}, device_id_type=pl.DeviceIdType.MESH
        )
    for offset in range(1, chips):
        pl.semaphore_signal(
            barrier,
            inc=1,
            device_id={"prompt": chip_peer(offset)},
            device_id_type=pl.DeviceIdType.MESH,
        )
    pl.semaphore_signal(
        barrier, inc=1, device_id={"prompt": partner}, device_id_type=pl.DeviceIdType.MESH
    )
    pl.semaphore_wait(barrier, seq_size - 1 + chips - 1 + 1)

    def token_rows(owner):
        return pl.ds(pl.multiple_of(owner * tokens, tokens), tokens)

    def text_rows(owner):
        text = ctx_hbm.shape[0]
        return pl.ds(pl.multiple_of(owner * text, text), text)

    def head_columns(owner):
        return pl.ds(pl.multiple_of(owner * width, width), width)

    def weight_rows(owner):
        return pl.ds(pl.multiple_of(owner * depth, depth), depth)

    sources = {Q: q_hbm, K: k_hbm, V: v_hbm, CTX: ctx_hbm, CQ: cq_hbm}
    buffers = {Q: q_buf, K: k_buf, V: v_buf, CTX: ctx_buf, CQ: cq_buf}

    def piece(which, owner):
        if which == CTX:
            return sources[which]
        return sources[which].at[:, head_columns(owner)]

    def landing(which, owner):
        rows = text_rows(owner) if which == CTX else token_rows(owner)
        return buffers[which].at[rows]

    def seq_copy(which, offset):
        return pltpu.make_async_remote_copy(
            src_ref=piece(which, seq_peer(offset)),
            dst_ref=landing(which, seq),
            send_sem=seq_send.at[which, offset],
            recv_sem=seq_recv.at[which, offset],
            device_id={"seq": seq_peer(offset)},
            device_id_type=pl.DeviceIdType.MESH,
        )

    def text_start_here(way, hop):
        if way == 0:
            return (seq >= hop) & (seq + 1 < seq_size)
        return (seq + hop < seq_size) & (seq >= 1)

    def text_lands_here(way, hop):
        return seq >= hop + 1 if way == 0 else seq + 1 + hop < seq_size

    def text_copy(way, hop):
        owner = seq - hop if way == 0 else seq + hop
        peer = seq_peer(1 if way == 0 else seq_size - 1)
        rows = text_rows(owner)
        return pltpu.make_async_remote_copy(
            src_ref=ctx_hbm if hop == 0 else ctx_buf.at[rows],
            dst_ref=ctx_buf.at[rows],
            send_sem=text_send.at[way, hop],
            recv_sem=text_recv.at[way, hop],
            device_id={"seq": peer},
            device_id_type=pl.DeviceIdType.MESH,
        )

    def start_text(hop):
        for way in range(2):

            @pl.when(text_start_here(way, hop))
            def _():
                text_copy(way, hop).start()

    def wait_text(hop):
        for way in range(2):

            @pl.when(text_lands_here(way, hop))
            def _():
                text_copy(way, hop).wait_recv()

    weights = ((wk_hbm, wk_buf), (wv_hbm, wv_buf))

    def chip_copy(which, offset):
        shard, gathered = weights[which]
        return pltpu.make_async_remote_copy(
            src_ref=shard,
            dst_ref=gathered.at[weight_rows(prompt)],
            send_sem=chip_send.at[which, offset],
            recv_sem=chip_recv.at[which, offset],
            device_id={"prompt": chip_peer(offset)},
            device_id_type=pl.DeviceIdType.MESH,
        )

    def pair_copy(which, offset):
        shard, gathered = weights[which]
        rows = weight_rows(chip_source(offset))
        return pltpu.make_async_remote_copy(
            src_ref=shard if offset == 0 else gathered.at[rows],
            dst_ref=gathered.at[rows],
            send_sem=pair_send.at[which, offset],
            recv_sem=pair_recv.at[which, offset],
            device_id={"prompt": partner},
            device_id_type=pl.DeviceIdType.MESH,
        )

    def out_copy(offset, half):
        part = width // 2
        sent = pl.ds(half * part, part)
        landed = pl.ds(pl.multiple_of(seq * width + half * part, part), part)
        return pltpu.make_async_remote_copy(
            src_ref=out_buf.at[token_rows(seq_source(offset)), sent],
            dst_ref=out_hbm.at[:, landed],
            send_sem=out_send.at[offset, half],
            recv_sem=out_recv.at[offset, half],
            device_id={"seq": seq_source(offset)},
            device_id_type=pl.DeviceIdType.MESH,
        )

    offsets = range(1, seq_size)

    def start_pieces(*group):
        for offset in sorted(offsets, key=lambda offset: abs(2 * offset - seq_size)):
            for which in group:
                seq_copy(which, offset).start()

    groups = [[], [], [(K,), (V,), (Q,), (CQ,)]]
    start_text(0)
    for group in groups[0]:
        start_pieces(*group)
    for which in range(2):
        for offset in range(1, chips):
            chip_copy(which, offset).start()
    local_copies = [
        pltpu.make_async_copy(
            piece(which, seq), landing(which, seq), local_sem.at[which]
        )
        for which in (Q, K, V, CTX, CQ)
    ] + [
        pltpu.make_async_copy(
            weights[which][0], weights[which][1].at[weight_rows(prompt)], local_sem.at[5 + which]
        )
        for which in range(2)
    ]
    for copy in local_copies:
        copy.start()
    for which in range(2):
        pair_copy(which, 0).start()
    for copy in local_copies:
        copy.wait()

    def head_attend(query, key, value, length):
        scores = lax.dot_general(
            query, key, (((1,), (1,)), ((), ())), preferred_element_type=jnp.float32
        )
        if length is not None:
            slot = lax.broadcasted_iota(jnp.int32, scores.shape, 1)
            scores = jnp.where(slot < length, scores, -jnp.inf)
        row_max = jnp.max(scores, axis=1, keepdims=True)
        exps = jnp.exp((scores - row_max) * scaling)
        totals = jnp.sum(exps, axis=1, keepdims=True)
        mixed = jnp.dot(exps.astype(jnp.bfloat16), value, preferred_element_type=jnp.float32)
        return (mixed / totals).astype(jnp.bfloat16)

    def forward(which):
        for offset in range(1, chips):
            chip_copy(which, offset).wait_recv()
            pair_copy(which, offset).start()

    hops = seq_size - 1
    for hop in range(hops):
        wait_text(hop)
        if hop + 1 < hops:
            start_text(hop + 1)
        for group in sum(groups[hop + 1 : hop + 2], []):
            start_pieces(*group)
        if hop == min(1, hops - 1):
            forward(0)
    for group in sum(groups[hops + 1 :], []):
        start_pieces(*group)

    def project(which, target):
        for offset in range(chips):
            pair_copy(which, offset).wait_recv()
        gathered = weights[which][1]
        tile = math.gcd(width, 256)

        def column_tile(index, carry):
            columns = pl.ds(pl.multiple_of(index * tile, tile), tile)
            target[:, columns] = jnp.dot(
                ctx_buf[...], gathered[:, columns], preferred_element_type=jnp.float32
            ).astype(jnp.bfloat16)
            return carry

        lax.fori_loop(0, width // tile, column_tile, 0)

    project(0, text_keys)
    forward(1)
    project(1, text_values)
    for which in (K, V, Q):
        for offset in offsets:
            seq_copy(which, offset).wait_recv()

    def self_head(head, carry):
        columns = pl.ds(pl.multiple_of(head * HD, HD), HD)
        key = k_buf[:, columns]
        value = v_buf[:, columns]

        def block(index, inner):
            rows = token_rows(index)
            self_buf[rows, columns] = head_attend(q_buf[rows, columns], key, value, None)
            return inner

        return lax.fori_loop(0, seq_size, block, carry)

    lax.fori_loop(0, heads, self_head, 0)
    length = length_ref[0]

    arrival = sorted(offsets, key=lambda offset: abs(2 * offset - seq_size))
    for offset in arrival + [0]:
        if offset:
            seq_copy(CQ, offset).wait_recv()
        rows = token_rows(seq_source(offset))

        def head_block(head, carry):
            columns = pl.ds(pl.multiple_of(head * HD, HD), HD)
            alone = self_buf[rows, columns]
            part = head_attend(
                cq_buf[rows, columns], text_keys[:, columns], text_values[:, columns], length
            )
            out_buf[rows, columns] = (
                alone.astype(jnp.float32) + part.astype(jnp.float32)
            ).astype(jnp.bfloat16)
            return carry

        for half in range(2):
            lax.fori_loop(half * (heads // 2), (half + 1) * (heads // 2), head_block, 0)
            if offset:
                out_copy(offset, half).start()
    own = pltpu.make_async_copy(
        out_buf.at[token_rows(seq)], out_hbm.at[:, head_columns(seq)], local_sem.at[7]
    )
    own.start()

    for which in (Q, K, V, CQ):
        for offset in offsets:
            seq_copy(which, offset).wait_send()
    for hop in range(hops):
        for way in range(2):

            @pl.when(text_start_here(way, hop))
            def _():
                text_copy(way, hop).wait_send()

    for which in range(2):
        for offset in range(1, chips):
            chip_copy(which, offset).wait_send()
        for offset in range(chips):
            pair_copy(which, offset).wait_send()
    own.wait()
    for offset in offsets:
        for half in range(2):
            out_copy(offset, half).wait()


def body(
    seq_size,
    prompt_size,
    queries,
    self_keys,
    self_values,
    cross_queries,
    context,
    key_weight,
    value_weight,
    lengths,
):
    tokens = queries.shape[1]
    full = tokens * seq_size
    width = key_weight.shape[1]
    model = context.shape[2]
    chips = prompt_size // CORES
    text_full = context.shape[1] * seq_size
    activations = pltpu.VMEM((full, width), jnp.bfloat16)
    texts = pltpu.VMEM((text_full, width), jnp.bfloat16)
    dma = pltpu.SemaphoreType.DMA
    attended = pl.pallas_call(
        functools.partial(kernel, seq_size, prompt_size),
        out_shape=jax.ShapeDtypeStruct(queries.shape[1:], jnp.bfloat16),
        in_specs=[pl.BlockSpec(memory_space=pltpu.SMEM)]
        + [pl.BlockSpec(memory_space=pl.ANY)] * 7,
        out_specs=pl.BlockSpec(memory_space=pl.ANY),
        scratch_shapes=[activations] * 4
        + [pltpu.VMEM((text_full, model), jnp.bfloat16)]
        + [pltpu.VMEM((model, width), jnp.bfloat16)] * 2
        + [texts] * 2
        + [activations] * 2
        + [
            dma((8,)),
            dma((5, seq_size)),
            dma((5, seq_size)),
            dma((2, seq_size)),
            dma((2, seq_size)),
            dma((2, chips)),
            dma((2, chips)),
            dma((2, chips)),
            dma((2, chips)),
            dma((seq_size, 2)),
            dma((seq_size, 2)),
        ],
        compiler_params=pltpu.CompilerParams(
            collective_id=0, has_side_effects=True, vmem_limit_bytes=60 * 1024 * 1024
        ),
    )(
        lengths,
        queries[0],
        self_keys[0],
        self_values[0],
        cross_queries[0],
        context[0],
        key_weight,
        value_weight,
    )
    return attended[None]


def solution(mesh):
    in_specs = (
        P("prompt", "seq", None),
        P("prompt", "seq", None),
        P("prompt", "seq", None),
        P("prompt", "seq", None),
        P("prompt", "seq", None),
        P("prompt", "seq"),
        P("prompt", "seq"),
        P("prompt"),
    )
    out_specs = P("prompt", "seq", None)
    step = functools.partial(body, mesh.shape["seq"], mesh.shape["prompt"])
    return jax.shard_map(step, mesh=mesh, in_specs=in_specs, out_specs=out_specs, check_vma=False)
```

profile of v0, /device:TPU:0, one launch (start us, length us, event | category | flops | bytes accessed | tf_op | source)
XLA Modules:
  0.0 191.9 jit_solution(3631411309548741085)
XLA Ops:
  0.7 189.0 %shard_map.82 = bf16[128,4096]{1,0:T(8,128)(2,1)} custom-call(s32[1]{0:T(128)S(6)} %copy.10.length_ref, bf16[128,4096]{1,0:T(8,128)(2,1)} %bitcast.8, bf16[128,4096]{1,0:T(8,128)(2,1)} %bitcast.9, bf16[128,4096]{1,0:T(8,128)(2,1)} %bitcast.10, bf16[128,4096]{1,0:T(8,128)(2,1)} %bitcast.11, bf16[128,5120]{1,0:T(8,128)(2,1)} %bitcast.7, ...), custom_call_target="tpu_custom_call" | custom-call | tf_op jit(solution)/shard_map/pallas_call | solution.py:367
  189.6 2.3 %copy.11 = bf16[1,128,4096]{2,1,0:T(8,128)(2,1)} copy(bf16[1,128,4096]{2,1,0:T(8,128)(2,1)} %bitcast.6) | data formatting | bytes 2097152
where the time goes:
time: 192 us
  Pallas kernels  189 us (98%)
  local copies, waits for them, and re-layouts  2.29 us (1%)
    pallas_call x1, Pallas kernels, body(): pl.pallas_call(functools.partial(kernel, seq_size, prompt_size), out_shap...  189 us

commit v1 on v0

v1 whole, which is shorter than its diff:
```python
import functools
import math

import jax
import jax.numpy as jnp
from jax import lax
from jax.experimental import pallas as pl
from jax.experimental.pallas import tpu as pltpu
from jax.sharding import PartitionSpec as P

HD = 128
CORES = 2
Q, K, V, CQ = range(4)
INPUTS = (K, V, Q, CQ)
SCORES = 512 * 512


TEXT_ROWS = 16


def group_heads(heads):
    return math.gcd(heads, 2) if heads > 2 else 1


def text_chunk(rows):
    return math.gcd(rows, TEXT_ROWS)


def kernel(
    seq_size,
    prompt_size,
    length_ref,
    q_hbm,
    k_hbm,
    v_hbm,
    cq_hbm,
    ctx_hbm,
    wk_hbm,
    wv_hbm,
    out_hbm,
    q_buf,
    k_buf,
    v_buf,
    cq_buf,
    ctx_buf,
    wk_buf,
    wv_buf,
    text_keys,
    text_values,
    self_buf,
    out_buf,
    local_sem,
    seq_send,
    seq_recv,
    text_send,
    text_recv,
    chip_send,
    chip_recv,
    pair_send,
    pair_recv,
    out_send,
    out_recv,
):
    seq = lax.axis_index("seq")
    prompt = lax.axis_index("prompt")
    chips = prompt_size // CORES
    chip = prompt // CORES
    core = prompt % CORES
    partner = chip * CORES + (1 - core)
    tokens = q_hbm.shape[0]
    text = ctx_hbm.shape[0]
    width = wk_hbm.shape[1]
    depth = wk_hbm.shape[0]
    heads = width // HD
    part = group_heads(heads) * HD
    groups = width // part
    chunk = text_chunk(text)
    chunks = text // chunk
    scaling = 1.0 / math.sqrt(HD)

    def seq_peer(offset):
        return lax.rem(seq + offset, seq_size)

    def seq_source(offset):
        return lax.rem(seq + seq_size - offset, seq_size)

    def chip_peer(offset):
        return lax.rem(chip + offset, chips) * CORES + core

    def chip_source(offset):
        return lax.rem(chip + chips - offset, chips) * CORES + core

    barrier = pltpu.get_barrier_semaphore()
    for offset in range(1, seq_size):
        pl.semaphore_signal(
            barrier, inc=1, device_id={"seq": seq_peer(offset)}, device_id_type=pl.DeviceIdType.MESH
        )
    for offset in range(1, chips):
        pl.semaphore_signal(
            barrier,
            inc=1,
            device_id={"prompt": chip_peer(offset)},
            device_id_type=pl.DeviceIdType.MESH,
        )
    pl.semaphore_signal(
        barrier, inc=1, device_id={"prompt": partner}, device_id_type=pl.DeviceIdType.MESH
    )
    pl.semaphore_wait(barrier, seq_size - 1 + chips - 1 + 1)

    def token_rows(owner):
        return pl.ds(pl.multiple_of(owner * tokens, tokens), tokens)

    def text_rows(owner):
        return pl.ds(pl.multiple_of(owner * text, text), text)

    def group_columns(group):
        return pl.ds(pl.multiple_of(group * part, part), part)

    def head_columns(owner, group):
        return pl.ds(pl.multiple_of(owner * width + group * part, part), part)

    def weight_rows(owner):
        return pl.ds(pl.multiple_of(owner * depth, depth), depth)

    sources = {Q: q_hbm, K: k_hbm, V: v_hbm, CQ: cq_hbm}
    buffers = {Q: q_buf, K: k_buf, V: v_buf, CQ: cq_buf}

    def seq_copy(which, group, offset):
        return pltpu.make_async_remote_copy(
            src_ref=sources[which].at[:, head_columns(seq_peer(offset), group)],
            dst_ref=buffers[which].at[token_rows(seq), group_columns(group)],
            send_sem=seq_send.at[which, group, offset],
            recv_sem=seq_recv.at[which, group, offset],
            device_id={"seq": seq_peer(offset)},
            device_id_type=pl.DeviceIdType.MESH,
        )

    def text_start_here(way, hop):
        if way == 0:
            return (seq >= hop) & (seq + 1 < seq_size)
        return (seq + hop < seq_size) & (seq >= 1)

    def text_lands_here(way, hop):
        return seq >= hop + 1 if way == 0 else seq + 1 + hop < seq_size

    def text_copy(way, hop, index):
        owner = seq - hop if way == 0 else seq + hop
        peer = seq_peer(1 if way == 0 else seq_size - 1)
        start = pl.multiple_of(index * chunk, chunk)
        rows = pl.ds(pl.multiple_of(owner * text + start, chunk), chunk)
        return pltpu.make_async_remote_copy(
            src_ref=ctx_hbm.at[pl.ds(start, chunk)] if hop == 0 else ctx_buf.at[rows],
            dst_ref=ctx_buf.at[rows],
            send_sem=text_send.at[way, hop, index],
            recv_sem=text_recv.at[way, hop, index],
            device_id={"seq": peer},
            device_id_type=pl.DeviceIdType.MESH,
        )

    def loop(count, step):
        def one(index, carry):
            step(index)
            return carry

        lax.fori_loop(0, count, one, 0)

    def start_text(way, hop, index):
        @pl.when(text_start_here(way, hop))
        def _():
            text_copy(way, hop, index).start()

    def wait_text(way, hop, index):
        @pl.when(text_lands_here(way, hop))
        def _():
            text_copy(way, hop, index).wait_recv()

    def relay_text(hop):
        def step(index):
            for way in range(2):
                if hop:
                    wait_text(way, hop - 1, index)
                if hop < hops:
                    start_text(way, hop, index)

        loop(chunks, step)

    weights = ((wk_hbm, wk_buf), (wv_hbm, wv_buf))

    def chip_copy(which, offset):
        shard, gathered = weights[which]
        return pltpu.make_async_remote_copy(
            src_ref=shard,
            dst_ref=gathered.at[weight_rows(prompt)],
            send_sem=chip_send.at[which, offset],
            recv_sem=chip_recv.at[which, offset],
            device_id={"prompt": chip_peer(offset)},
            device_id_type=pl.DeviceIdType.MESH,
        )

    def pair_copy(which, offset):
        shard, gathered = weights[which]
        rows = weight_rows(chip_source(offset))
        return pltpu.make_async_remote_copy(
            src_ref=shard if offset == 0 else gathered.at[rows],
            dst_ref=gathered.at[rows],
            send_sem=pair_send.at[which, offset],
            recv_sem=pair_recv.at[which, offset],
            device_id={"prompt": partner},
            device_id_type=pl.DeviceIdType.MESH,
        )

    def out_copy(offset, group):
        return pltpu.make_async_remote_copy(
            src_ref=out_buf.at[token_rows(seq_source(offset)), group_columns(group)],
            dst_ref=out_hbm.at[:, head_columns(seq, group)],
            send_sem=out_send.at[group, offset],
            recv_sem=out_recv.at[group, offset],
            device_id={"seq": seq_source(offset)},
            device_id_type=pl.DeviceIdType.MESH,
        )

    offsets = sorted(range(1, seq_size), key=lambda offset: abs(2 * offset - seq_size))
    hops = seq_size - 1

    def relays_left(offset):
        right = text_start_here(0, 2)
        left = text_start_here(1, 2)
        ahead = seq + offset < seq_size
        return (ahead & right) | (jnp.logical_not(ahead) & left)

    def start_inputs(late):
        def group_step(group):
            for offset in offsets:

                @pl.when(relays_left(offset) == late)
                def _():
                    for which in INPUTS:
                        seq_copy(which, group, offset).start()

        loop(groups, group_step)

    relay_text(0)
    for which in range(2):
        for offset in range(1, chips):
            chip_copy(which, offset).start()
    for which in range(2):
        pair_copy(which, 0).start()
    own_columns = pl.ds(pl.multiple_of(seq * width, width), width)
    local_copies = [
        pltpu.make_async_copy(
            sources[which].at[:, own_columns], buffers[which].at[token_rows(seq)], local_sem.at[which]
        )
        for which in INPUTS
    ] + [
        pltpu.make_async_copy(ctx_hbm, ctx_buf.at[text_rows(seq)], local_sem.at[4]),
        pltpu.make_async_copy(wk_hbm, wk_buf.at[weight_rows(prompt)], local_sem.at[5]),
        pltpu.make_async_copy(wv_hbm, wv_buf.at[weight_rows(prompt)], local_sem.at[6]),
    ]
    for copy in local_copies:
        copy.start()

    def attend(query, key, value, length):
        scores = lax.dot_general(
            query, key, (((1,), (1,)), ((), ())), preferred_element_type=jnp.float32
        )
        if length is not None:
            slot = lax.broadcasted_iota(jnp.int32, scores.shape, 1)
            scores = jnp.where(slot < length, scores, -jnp.inf)
        row_max = jnp.max(scores, axis=1, keepdims=True)
        exps = jnp.exp((scores - row_max) * scaling)
        totals = jnp.sum(exps, axis=1, keepdims=True)
        mixed = jnp.dot(exps.astype(jnp.bfloat16), value, preferred_element_type=jnp.float32)
        return (mixed / totals).astype(jnp.bfloat16)

    def row_blocks(keys):
        full = tokens * seq_size
        block = full
        while block > tokens and (block * keys > SCORES or full % block):
            block //= 2
        return block, full // block

    def over_rows(keys, step):
        block, count = row_blocks(keys)
        if count == 1:
            step(slice(None))
        else:
            loop(count, lambda index: step(pl.ds(pl.multiple_of(index * block, block), block)))

    def over_heads(group, step):
        def head(index):
            step(pl.ds(pl.multiple_of(group * part + index * HD, HD), HD))

        loop(part // HD, head)

    def self_group(group):
        for which in (K, V, Q):
            for offset in offsets:
                seq_copy(which, group, offset).wait_recv()

        def head(columns):
            key = k_buf[:, columns]
            value = v_buf[:, columns]

            def block(rows):
                self_buf[rows, columns] = attend(q_buf[rows, columns], key, value, None)

            over_rows(k_buf.shape[0], block)

        over_heads(group, head)

    def cross_group(group):
        for offset in offsets:
            seq_copy(CQ, group, offset).wait_recv()
        length = length_ref[0]

        def head(columns):
            key = text_keys[:, columns]
            value = text_values[:, columns]

            def block(rows):
                part = attend(cq_buf[rows, columns], key, value, length)
                out_buf[rows, columns] = (
                    self_buf[rows, columns].astype(jnp.float32) + part.astype(jnp.float32)
                ).astype(jnp.bfloat16)

            over_rows(text_keys.shape[0], block)

        over_heads(group, head)
        for offset in offsets:
            out_copy(offset, group).start()

    def forward(which):
        for offset in range(1, chips):
            chip_copy(which, offset).wait_recv()
            pair_copy(which, offset).start()

    def project(which, target):
        for offset in range(chips):
            pair_copy(which, offset).wait_recv()
        gathered = weights[which][1]
        tile = math.gcd(width, 256)

        def column_tile(index):
            columns = pl.ds(pl.multiple_of(index * tile, tile), tile)
            target[:, columns] = jnp.dot(
                ctx_buf[...], gathered[:, columns], preferred_element_type=jnp.float32
            ).astype(jnp.bfloat16)

        loop(width // tile, column_tile)

    relay_text(1)
    for copy in local_copies:
        copy.wait()
    start_inputs(False)
    for hop in range(2, hops):
        relay_text(hop)
    start_inputs(True)
    forward(0)
    for hop in range(max(hops, 2), hops + 1):
        relay_text(hop)
    project(0, text_keys)
    early = groups // 2
    loop(early, self_group)
    forward(1)
    project(1, text_values)
    loop(early, cross_group)

    def late_group(index):
        self_group(early + index)
        cross_group(early + index)

    loop(groups - early, late_group)
    own = pltpu.make_async_copy(
        out_buf.at[token_rows(seq)], out_hbm.at[:, own_columns], local_sem.at[7]
    )
    own.start()

    def sent_group(group):
        for which in INPUTS:
            for offset in offsets:
                seq_copy(which, group, offset).wait_send()

    loop(groups, sent_group)

    def sent_text(index):
        for hop in range(hops):
            for way in range(2):

                @pl.when(text_start_here(way, hop))
                def _():
                    text_copy(way, hop, index).wait_send()

    loop(chunks, sent_text)
    for which in range(2):
        for offset in range(1, chips):
            chip_copy(which, offset).wait_send()
        for offset in range(chips):
            pair_copy(which, offset).wait_send()
    own.wait()

    def out_group(group):
        for offset in offsets:
            out_copy(offset, group).wait()

    loop(groups, out_group)


def body(
    seq_size,
    prompt_size,
    queries,
    self_keys,
    self_values,
    cross_queries,
    context,
    key_weight,
    value_weight,
    lengths,
):
    tokens = queries.shape[1]
    full = tokens * seq_size
    width = key_weight.shape[1]
    model = context.shape[2]
    chips = prompt_size // CORES
    text_full = context.shape[1] * seq_size
    groups = width // HD // group_heads(width // HD)
    chunks = context.shape[1] // text_chunk(context.shape[1])
    activations = pltpu.VMEM((full, width), jnp.bfloat16)
    texts = pltpu.VMEM((text_full, width), jnp.bfloat16)
    dma = pltpu.SemaphoreType.DMA
    attended = pl.pallas_call(
        functools.partial(kernel, seq_size, prompt_size),
        out_shape=jax.ShapeDtypeStruct(queries.shape[1:], jnp.bfloat16),
        in_specs=[pl.BlockSpec(memory_space=pltpu.SMEM)]
        + [pl.BlockSpec(memory_space=pl.ANY)] * 7,
        out_specs=pl.BlockSpec(memory_space=pl.ANY),
        scratch_shapes=[activations] * 4
        + [pltpu.VMEM((text_full, model), jnp.bfloat16)]
        + [pltpu.VMEM((model, width), jnp.bfloat16)] * 2
        + [texts] * 2
        + [activations] * 2
        + [
            dma((8,)),
            dma((4, groups, seq_size)),
            dma((4, groups, seq_size)),
            dma((2, seq_size, chunks)),
            dma((2, seq_size, chunks)),
            dma((2, chips)),
            dma((2, chips)),
            dma((2, chips)),
            dma((2, chips)),
            dma((groups, seq_size)),
            dma((groups, seq_size)),
        ],
        compiler_params=pltpu.CompilerParams(
            collective_id=0, has_side_effects=True, vmem_limit_bytes=60 * 1024 * 1024
        ),
    )(
        lengths,
        queries[0],
        self_keys[0],
        self_values[0],
        cross_queries[0],
        context[0],
        key_weight,
        value_weight,
    )
    return attended[None]


def solution(mesh):
    in_specs = (
        P("prompt", "seq", None),
        P("prompt", "seq", None),
        P("prompt", "seq", None),
        P("prompt", "seq", None),
        P("prompt", "seq", None),
        P("prompt", "seq"),
        P("prompt", "seq"),
        P("prompt"),
    )
    out_specs = P("prompt", "seq", None)
    step = functools.partial(body, mesh.shape["seq"], mesh.shape["prompt"])
    return jax.shard_map(step, mesh=mesh, in_specs=in_specs, out_specs=out_specs, check_vma=False)
```

time: 192 us -> 181 us (0.943)
  Pallas kernels: 189 us -> 178 us
    pallas_call x1, Pallas kernels: 189 us -> 178 us  [body(): pl.pallas_call(functools.partial(kernel, seq_size, prompt_size), out_shap...]
where the time goes in v1:
time: 181 us
  Pallas kernels  178 us (98%)
  local copies, waits for them, and re-layouts  2.29 us (1%)
    pallas_call x1, Pallas kernels, body(): pl.pallas_call(functools.partial(kernel, seq_size, prompt_size), out_shap...  178 us

profile of v1, /device:TPU:0, one launch (start us, length us, event | category | flops | bytes accessed | tf_op | source)
XLA Modules:
  0.0 180.9 jit_solution(10751418544321019362)
XLA Ops:
  0.7 178.0 %shard_map.82 = bf16[128,4096]{1,0:T(8,128)(2,1)} custom-call(s32[1]{0:T(128)S(6)} %copy.10.length_ref, bf16[128,4096]{1,0:T(8,128)(2,1)} %bitcast.8, bf16[128,4096]{1,0:T(8,128)(2,1)} %bitcast.9, bf16[128,4096]{1,0:T(8,128)(2,1)} %bitcast.10, bf16[128,4096]{1,0:T(8,128)(2,1)} %bitcast.11, bf16[128,5120]{1,0:T(8,128)(2,1)} %bitcast.7, ...), custom_call_target="tpu_custom_call" | custom-call | tf_op jit(solution)/shard_map/pallas_call | solution.py:431
  178.6 2.3 %copy.11 = bf16[1,128,4096]{2,1,0:T(8,128)(2,1)} copy(bf16[1,128,4096]{2,1,0:T(8,128)(2,1)} %bitcast.6) | data formatting | bytes 2097152

commit v2 on v1

--- a/solution.py
+++ b/solution.py
@@ -60,6 +60,8 @@
     pair_recv,
     out_send,
     out_recv,
+    seq_sem,
+    chip_sem,
 ):
     seq = lax.axis_index("seq")
     prompt = lax.axis_index("prompt")
@@ -84,28 +86,72 @@
     def seq_source(offset):
         return lax.rem(seq + seq_size - offset, seq_size)
 
+    folds = [1 << bit for bit in range(chips.bit_length() - 1)] if chips & (chips - 1) == 0 else []
+
     def chip_peer(offset):
-        return lax.rem(chip + offset, chips) * CORES + core
+        if not folds:
+            return lax.rem(chip + offset, chips) * CORES + core
+        peer = chip
+        for fold in folds:
+            if offset & fold:
+                peer = peer + fold * (1 - 2 * ((peer // fold) % 2))
+        return peer * CORES + core
 
     def chip_source(offset):
-        return lax.rem(chip + chips - offset, chips) * CORES + core
-
-    barrier = pltpu.get_barrier_semaphore()
-    for offset in range(1, seq_size):
+        return chip_peer(offset if folds else chips - offset)
+
+    def seq_greet(semaphores, reach):
+        for way, step in enumerate((reach, -reach)):
+
+            @pl.when((seq + step >= 0) & (seq + step < seq_size))
+            def _():
+                pl.semaphore_signal(
+                    semaphores(way),
+                    inc=1,
+                    device_id={"seq": seq + step},
+                    device_id_type=pl.DeviceIdType.MESH,
+                )
+
+    def seq_met(semaphore, way, reach):
+        step = -reach if way == 0 else reach
+
+        @pl.when((seq + step >= 0) & (seq + step < seq_size))
+        def _():
+            pl.semaphore_wait(semaphore, 1)
+
+    def chip_greet(semaphore, offset):
         pl.semaphore_signal(
-            barrier, inc=1, device_id={"seq": seq_peer(offset)}, device_id_type=pl.DeviceIdType.MESH
-        )
-    for offset in range(1, chips):
-        pl.semaphore_signal(
-            barrier,
+            semaphore,
             inc=1,
             device_id={"prompt": chip_peer(offset)},
             device_id_type=pl.DeviceIdType.MESH,
         )
+
+    near = folds if folds else list(range(1, chips))
+    barrier = pltpu.get_barrier_semaphore()
+    seq_greet(lambda way: barrier, 1)
+    for offset in near:
+        chip_greet(barrier, offset)
     pl.semaphore_signal(
         barrier, inc=1, device_id={"prompt": partner}, device_id_type=pl.DeviceIdType.MESH
     )
-    pl.semaphore_wait(barrier, seq_size - 1 + chips - 1 + 1)
+    inner = jnp.where(seq == 0, 0, 1) + jnp.where(seq == seq_size - 1, 0, 1)
+    pl.semaphore_wait(barrier, inner + len(near) + 1)
+
+    def meet_seq():
+        reach, turn = 1, 0
+        while reach < seq_size - 1:
+            seq_greet(lambda way: seq_sem.at[turn, way], reach)
+            for way in range(2):
+                seq_met(seq_sem.at[turn, way], way, reach)
+            reach, turn = 2 * reach, turn + 1
+
+    def meet_chips():
+        for turn in range(len(folds) - 1):
+            for index, fold in enumerate(folds):
+                chip_greet(chip_sem.at[turn, index], fold)
+            for index, fold in enumerate(folds):
+                pl.semaphore_wait(chip_sem.at[turn, index], 1)
 
     def token_rows(owner):
         return pl.ds(pl.multiple_of(owner * tokens, tokens), tokens)
@@ -240,9 +286,14 @@
         loop(groups, group_step)
 
     relay_text(0)
+    for offset in near:
+        chip_copy(0, offset).start()
+    meet_seq()
+    meet_chips()
     for which in range(2):
         for offset in range(1, chips):
-            chip_copy(which, offset).start()
+            if which or offset not in near:
+                chip_copy(which, offset).start()
     for which in range(2):
         pair_copy(which, 0).start()
     own_columns = pl.ds(pl.multiple_of(seq * width, width), width)
@@ -432,7 +483,7 @@
         functools.partial(kernel, seq_size, prompt_size),
         out_shape=jax.ShapeDtypeStruct(queries.shape[1:], jnp.bfloat16),
         in_specs=[pl.BlockSpec(memory_space=pltpu.SMEM)]
-        + [pl.BlockSpec(memory_space=pl.ANY)] * 7,
+        + [pl.BlockSpec(memory_space=pltpu.HBM)] * 7,
         out_specs=pl.BlockSpec(memory_space=pl.ANY),
         scratch_shapes=[activations] * 4
         + [pltpu.VMEM((text_full, model), jnp.bfloat16)]
@@ -451,19 +502,26 @@
             dma((2, chips)),
             dma((groups, seq_size)),
             dma((groups, seq_size)),
+            pltpu.SemaphoreType.REGULAR((seq_size.bit_length(), 2)),
+            pltpu.SemaphoreType.REGULAR((chips.bit_length(), chips.bit_length())),
         ],
         compiler_params=pltpu.CompilerParams(
-            collective_id=0, has_side_effects=True, vmem_limit_bytes=60 * 1024 * 1024
+            collective_id=0, has_side_effects=True, vmem_limit_bytes=48 * 1024 * 1024
         ),
     )(
         lengths,
-        queries[0],
-        self_keys[0],
-        self_values[0],
-        cross_queries[0],
-        context[0],
-        key_weight,
-        value_weight,
+        *(
+            pltpu.with_memory_space_constraint(operand, pltpu.HBM)
+            for operand in (
+                queries[0],
+                self_keys[0],
+                self_values[0],
+                cross_queries[0],
+                context[0],
+                key_weight,
+                value_weight,
+            )
+        ),
     )
     return attended[None]
 

time: 181 us -> 179 us (0.989)
  no operation moved by 1% of the time
where the time goes in v2:
time: 179 us
  Pallas kernels  177 us (99%)
    pallas_call x1, Pallas kernels, body(): pl.pallas_call(functools.partial(kernel, seq_size, prompt_size), out_shap...  177 us

profile of v2, /device:TPU:0, one launch (start us, length us, event | category | flops | bytes accessed | tf_op | source)
XLA Modules:
  0.0 178.9 jit_solution(3931602827128632290)
XLA Ops:
  0.7 177.3 %shard_map.82 = bf16[128,4096]{1,0:T(8,128)(2,1)S(1)} custom-call(s32[1]{0:T(128)S(6)} %copy.10.length_ref, bf16[128,4096]{1,0:T(8,128)(2,1)} %bitcast.8, bf16[128,4096]{1,0:T(8,128)(2,1)} %bitcast.9, bf16[128,4096]{1,0:T(8,128)(2,1)} %bitcast.10, bf16[128,4096]{1,0:T(8,128)(2,1)} %bitcast.11, bf16[128,5120]{1,0:T(8,128)(2,1)} %bitcast.7, ...), custom_call_target="tpu_custom_call" | custom-call | tf_op jit(solution)/shard_map/pallas_call | solution.py:482
  177.9 1.0 copy.11

commit v3 on v2

--- a/solution.py
+++ b/solution.py
@@ -49,6 +49,10 @@
     text_values,
     self_buf,
     out_buf,
+    aid_q,
+    aid_k,
+    aid_v,
+    aid_out,
     local_sem,
     seq_send,
     seq_recv,
@@ -62,6 +66,10 @@
     out_recv,
     seq_sem,
     chip_sem,
+    aid_send,
+    aid_recv,
+    aid_local,
+    aid_done,
 ):
     seq = lax.axis_index("seq")
     prompt = lax.axis_index("prompt")
@@ -181,6 +189,71 @@
             device_id_type=pl.DeviceIdType.MESH,
         )
 
+    aided = seq_size >= 4
+    at_end = (seq == 0) | (seq == seq_size - 1)
+    at_helper = (seq == 1) | (seq == seq_size - 2)
+    sides = ((0, 1), (seq_size - 1, seq_size - 2)) if aided else ()
+    aids = {Q: aid_q, K: aid_k, V: aid_v}
+
+    def to_end(offset):
+        peer = seq_peer(offset)
+        return (peer == 0) | (peer == seq_size - 1)
+
+    def aid_copy(which, side, source):
+        end, helper = sides[side]
+        return pltpu.make_async_remote_copy(
+            src_ref=sources[which].at[:, head_columns(end, 0)],
+            dst_ref=aids[which].at[token_rows(source)],
+            send_sem=aid_send.at[which, side],
+            recv_sem=aid_recv.at[which, source],
+            device_id={"seq": helper},
+            device_id_type=pl.DeviceIdType.MESH,
+        )
+
+    def aid_own(which, side):
+        return pltpu.make_async_copy(
+            sources[which].at[:, head_columns(sides[side][0], 0)],
+            aids[which].at[token_rows(seq)],
+            aid_local.at[which],
+        )
+
+    def aid_result():
+        return pltpu.make_async_remote_copy(
+            src_ref=aid_out,
+            dst_ref=self_buf.at[:, group_columns(0)],
+            send_sem=aid_done.at[0],
+            recv_sem=aid_done.at[1],
+            device_id={"seq": jnp.where(seq == 1, 0, seq_size - 1)},
+            device_id_type=pl.DeviceIdType.MESH,
+        )
+
+    def start_aid():
+        for side, (end, helper) in enumerate(sides):
+
+            @pl.when(seq != helper)
+            def _():
+                for which in (K, V, Q):
+                    aid_copy(which, side, seq).start()
+
+            @pl.when(seq == helper)
+            def _():
+                for which in (K, V, Q):
+                    aid_own(which, side).start()
+
+    def sent_aid():
+        for side, (end, helper) in enumerate(sides):
+
+            @pl.when(seq != helper)
+            def _():
+                for which in (K, V, Q):
+                    aid_copy(which, side, seq).wait_send()
+
+        if aided:
+
+            @pl.when(at_helper)
+            def _():
+                aid_result().wait_send()
+
     def text_start_here(way, hop):
         if way == 0:
             return (seq >= hop) & (seq + 1 < seq_size)
@@ -275,15 +348,31 @@
         return (ahead & right) | (jnp.logical_not(ahead) & left)
 
     def start_inputs(late):
-        def group_step(group):
-            for offset in offsets:
-
-                @pl.when(relays_left(offset) == late)
+        if not late:
+            start_aid()
+
+        def start_one(group, offset, valid):
+            @pl.when(valid & (relays_left(offset) == late))
+            def _():
+                @pl.when((group > 0) | jnp.logical_not(aided & to_end(offset)))
                 def _():
-                    for which in INPUTS:
+                    for which in (K, V, Q):
                         seq_copy(which, group, offset).start()
 
-        loop(groups, group_step)
+                seq_copy(CQ, group, offset).start()
+
+        batch = max(groups // 1, 1)
+
+        def batch_step(index):
+            for distance in range(1, seq_size):
+
+                def group_step(group):
+                    start_one(index * batch + group, distance, seq + distance < seq_size)
+                    start_one(index * batch + group, seq_size - distance, seq >= distance)
+
+                loop(batch, group_step)
+
+        loop(groups // batch, batch_step)
 
     relay_text(0)
     for offset in near:
@@ -359,6 +448,55 @@
 
         over_heads(group, head)
 
+    def aid_group():
+        @pl.when(at_helper)
+        def _():
+            for source in range(seq_size):
+
+                @pl.when(seq != source)
+                def _():
+                    for which in (K, V, Q):
+                        aid_copy(which, 0, source).wait_recv()
+
+            for side, (end, helper) in enumerate(sides):
+
+                @pl.when(seq == helper)
+                def _():
+                    for which in (K, V, Q):
+                        aid_own(which, side).wait()
+
+            def head(index):
+                columns = pl.ds(pl.multiple_of(index * HD, HD), HD)
+                key = aid_k[:, columns]
+                value = aid_v[:, columns]
+
+                def block(rows):
+                    aid_out[rows, columns] = attend(aid_q[rows, columns], key, value, None)
+
+                over_rows(aid_k.shape[0], block)
+
+            loop(part // HD, head)
+            aid_result().start()
+
+    def first_self():
+        if not aided:
+            self_group(0)
+            return
+        aid_group()
+
+        @pl.when(jnp.logical_not(at_end))
+        def _():
+            self_group(0)
+
+    def first_cross():
+        if aided:
+
+            @pl.when(at_end)
+            def _():
+                aid_result().wait_recv()
+
+        cross_group(0)
+
     def cross_group(group):
         for offset in offsets:
             seq_copy(CQ, group, offset).wait_recv()
@@ -403,35 +541,45 @@
     for copy in local_copies:
         copy.wait()
     start_inputs(False)
+    start_inputs(True)
     for hop in range(2, hops):
         relay_text(hop)
-    start_inputs(True)
     forward(0)
     for hop in range(max(hops, 2), hops + 1):
         relay_text(hop)
     project(0, text_keys)
-    early = groups // 2
-    loop(early, self_group)
+    early = max(groups // 2, 1)
+    first_self()
+    loop(early - 1, lambda index: self_group(1 + index))
     forward(1)
     project(1, text_values)
-    loop(early, cross_group)
-
-    def late_group(index):
-        self_group(early + index)
-        cross_group(early + index)
-
-    loop(groups - early, late_group)
+    loop(early - 1, lambda index: cross_group(1 + index))
+
+    def late_group(group):
+        self_group(group)
+        cross_group(group)
+
+    loop(groups - early - 1, lambda index: late_group(early + index))
+    first_cross()
+    if groups > early:
+        late_group(groups - 1)
     own = pltpu.make_async_copy(
         out_buf.at[token_rows(seq)], out_hbm.at[:, own_columns], local_sem.at[7]
     )
     own.start()
 
     def sent_group(group):
-        for which in INPUTS:
-            for offset in offsets:
-                seq_copy(which, group, offset).wait_send()
+        for offset in offsets:
+
+            @pl.when((group > 0) | jnp.logical_not(aided & to_end(offset)))
+            def _():
+                for which in (K, V, Q):
+                    seq_copy(which, group, offset).wait_send()
+
+            seq_copy(CQ, group, offset).wait_send()
 
     loop(groups, sent_group)
+    sent_aid()
 
     def sent_text(index):
         for hop in range(hops):
@@ -490,6 +638,7 @@
         + [pltpu.VMEM((model, width), jnp.bfloat16)] * 2
         + [texts] * 2
         + [activations] * 2
+        + [pltpu.VMEM((full, group_heads(width // HD) * HD), jnp.bfloat16)] * 4
         + [
             dma((8,)),
             dma((4, groups, seq_size)),
@@ -504,6 +653,10 @@
             dma((groups, seq_size)),
             pltpu.SemaphoreType.REGULAR((seq_size.bit_length(), 2)),
             pltpu.SemaphoreType.REGULAR((chips.bit_length(), chips.bit_length())),
+            dma((3, 2)),
+            dma((3, seq_size)),
+            dma((3,)),
+            dma((2,)),
         ],
         compiler_params=pltpu.CompilerParams(
             collective_id=0, has_side_effects=True, vmem_limit_bytes=48 * 1024 * 1024

time: 179 us -> 179 us (level)
  no operation moved by 1% of the time
where the time goes in v3:
time: 179 us; the launch traced here: 178 us
  Pallas kernels  177 us (99%)
    pallas_call x1, Pallas kernels, body(): pl.pallas_call(functools.partial(kernel, seq_size, prompt_size), out_shap...  177 us

profile of v3, /device:TPU:0, one launch (start us, length us, event | category | flops | bytes accessed | tf_op | source)
XLA Modules:
  0.0 178.4 jit_solution(9139124701191795622)
XLA Ops:
  0.7 176.8 %shard_map.82 = bf16[128,4096]{1,0:T(8,128)(2,1)S(1)} custom-call(s32[1]{0:T(128)S(6)} %copy.10.length_ref, bf16[128,4096]{1,0:T(8,128)(2,1)} %bitcast.8, bf16[128,4096]{1,0:T(8,128)(2,1)} %bitcast.9, bf16[128,4096]{1,0:T(8,128)(2,1)} %bitcast.10, bf16[128,4096]{1,0:T(8,128)(2,1)} %bitcast.11, bf16[128,5120]{1,0:T(8,128)(2,1)} %bitcast.7, ...), custom_call_target="tpu_custom_call" | custom-call | tf_op jit(solution)/shard_map/pallas_call | solution.py:630
  177.4 1.0 copy.11
